TPU v7x, 32 devices: a whole 2x2x4 slice. The times are simulated.
32 devices in a mesh: mem: 8 (over y, x, core), band: 4 (over z).
Axes of the slice: x: 2, y: 2, z: 4, core: 2. Of those that a mesh axis runs over, the one named last changes fastest.
Arguments:
- ensemble: bfloat16 [256, 3, 240, 160], P('mem', None, 'band'), may hold values from -8 to 8, as said below
- layer_depth: float32 [240, 160], P('band'), may hold values from 0.5 to 2
- observed_cell: int32 [8, 8, 512], P('mem', 'band'), may hold values from 0 to 1799
- observed_value: float32 [8, 8, 512], P('mem', 'band'), may hold values from -6 to 6
- error_variance: float32 [8, 8, 512], P('mem', 'band'), may hold values from 4 to 64
- observed_count: int32 [8, 8], P('mem', 'band'), may hold values from 256 to 512, as said below
Outputs:
- analysis: bfloat16 [256, 3, 240, 160], P('mem', None, 'band')
Inputs may be any that keep to these rules, and one draw needn't show every extreme that they name: `ensemble`: the forecast members scatter around a common state. `observed_count`: some tile holds 512 observations; the slots from the count on are unused.
All inputs are finite; a program needn't handle non-finite values.
Results may differ from a plain program's by a relative error of at most 0.0051.
The roundings to bfloat16 on the way count: a program that leaves them out, or rounds other values in their place, can miss the bound.
Values may be sent and summed in bfloat16 or wider, within the bound.
No kernel may reach another device: no remote copies, remote signals or barrier semaphores. Data moves between devices by JAX's collectives and lax.ppermute only.
A program may use at most 128 MiB of HBM per device.

v0:
```python
import math
import jax
import jax.numpy as jnp
from jax import lax
from jax.sharding import PartitionSpec as P

SWEEPS = 5
half_step = 0.1
coriolis_scale = 0.3
neighbour_weight = 0.75


def padded_2(cells, sides, width):
    for axis, dim in sides:
        count = lax.axis_size(axis)
        head = lax.slice_in_dim(cells, 0, width, axis=dim)
        tail = lax.slice_in_dim(cells, cells.shape[dim] - width, cells.shape[dim], axis=dim)
        cells = jnp.concatenate(
            [
                lax.ppermute(tail, axis, [(i, (i + 1) % count) for i in range(count)]),
                cells,
                lax.ppermute(head, axis, [((i + 1) % count, i) for i in range(count)]),
            ],
            axis=dim,
        )
    return cells


def north_south(source):
    widths = [(0, 0)] * (source.ndim - 1) + [(1, 1)]
    padded = jnp.pad(source, widths)
    return padded[..., 2:] - padded[..., :-2]


def coriolis(latitudes):
    position = jnp.arange(latitudes, dtype=jnp.float32)
    return coriolis_scale * jnp.sin(math.pi * ((position + 0.5) / latitudes - 0.5))


def newton_schulz(starting):
    identity = jnp.eye(starting.shape[-1], dtype=starting.dtype)
    root_part = starting
    inverse_root = jnp.broadcast_to(identity, starting.shape)
    for sweep_index in range(SWEEPS):
        product = jnp.einsum(
            "tij,tjk->tik", inverse_root, root_part, precision=lax.Precision.HIGHEST
        )
        middle = 1.5 * identity - 0.5 * product
        root_part = jnp.einsum("tij,tjk->tik", root_part, middle, precision=lax.Precision.HIGHEST)
        inverse_root = jnp.einsum(
            "tij,tjk->tik", middle, inverse_root, precision=lax.Precision.HIGHEST
        )
    return inverse_root


def on_device(ensemble, layer_depth, observed_cell, observed_value, error_variance, observed_count):
    block_members = ensemble.shape[0]
    columns = ensemble.shape[2]
    latitudes = ensemble.shape[3]
    strips = lax.axis_size("mem")
    members = block_members * strips
    strip_rows = latitudes // strips
    tile_count = observed_cell.shape[1]
    tile_columns = columns // tile_count
    slot_count = observed_cell.shape[2]
    tile_cells = 3 * tile_columns * strip_rows
    height = ensemble[:, 0].astype(jnp.float32)
    eastward = ensemble[:, 1].astype(jnp.float32)
    northward = ensemble[:, 2].astype(jnp.float32)
    turning = coriolis(latitudes)
    flux_east = (layer_depth * eastward).astype(jnp.bfloat16)
    flux_north = (layer_depth * northward).astype(jnp.bfloat16)
    east_margin = padded_2(flux_east, (("band", 1),), 1)
    east_west = east_margin[:, 2:].astype(jnp.float32) - east_margin[:, :-2].astype(jnp.float32)
    north_local = lax.optimization_barrier(flux_north).astype(jnp.float32)
    raised = height - half_step * (east_west + north_south(north_local))
    surface_elevation_cast = raised.astype(jnp.bfloat16)
    height_margin = padded_2(surface_elevation_cast, (("band", 1),), 1)
    margin_wide = height_margin.astype(jnp.float32)
    height_inner = margin_wide[:, 1:-1]
    revised_zonal_velocity = (
        eastward + turning * northward - half_step * (margin_wide[:, 2:] - margin_wide[:, :-2])
    )
    revised_meridional_velocity = (
        northward - turning * eastward - half_step * north_south(height_inner)
    )
    advance_dynamics = jnp.stack(
        [
            surface_elevation_cast,
            revised_zonal_velocity.astype(jnp.bfloat16),
            revised_meridional_velocity.astype(jnp.bfloat16),
        ],
        axis=1,
    )
    reordered = advance_dynamics.reshape(
        block_members, 3, tile_count, tile_columns, strips, strip_rows
    )
    reordered = jnp.transpose(reordered, (4, 2, 0, 1, 3, 5)).reshape(
        strips, tile_count, block_members, tile_cells
    )
    tile_block = lax.all_to_all(reordered, "mem", split_axis=0, concat_axis=2, tiled=True)[0]
    cells_here = observed_cell[0]
    values = jnp.take_along_axis(tile_block, cells_here[:, None, :], axis=2)
    observed_mean = jnp.sum(values, axis=1, dtype=jnp.float32) / members
    slot_index = jnp.arange(slot_count, dtype=jnp.int32)[None, :]
    live_slots = slot_index < observed_count[0][:, None]
    root_weight = jnp.sqrt(jnp.where(live_slots, 1.0 / error_variance[0], 0.0))
    spread = (
        root_weight[:, None, :] * (values.astype(jnp.float32) - observed_mean[:, None, :])
    ).astype(jnp.bfloat16)
    misfit = (root_weight * (observed_value[0] - observed_mean)).astype(jnp.bfloat16)
    spread_margin, misfit_margin = (
        padded_2(spread[None], (("mem", 0), ("band", 1)), 1),
        padded_2(misfit[None], (("mem", 0), ("band", 1)), 1),
    )
    gram_margin = jnp.einsum(
        "atko,atlo->atkl", spread_margin, spread_margin, preferred_element_type=jnp.float32
    )
    pull_margin = jnp.einsum(
        "atko,ato->atk", spread_margin, misfit_margin, preferred_element_type=jnp.float32
    )
    strip_here = lax.axis_index("mem")
    lower_valid = (strip_here > 0).astype(jnp.float32)
    upper_valid = (strip_here < strips - 1).astype(jnp.float32)
    strip_mask = (lower_valid, 1.0, upper_valid)
    total_gram = jnp.zeros((tile_count, members, members), jnp.float32)
    total_pull = jnp.zeros((tile_count, members), jnp.float32)
    for offset_lat in range(3):
        for offset_lon in range(3):
            factor = (
                neighbour_weight ** (abs(offset_lat - 1) + abs(offset_lon - 1))
                * strip_mask[offset_lat]
            )
            total_gram = (
                total_gram + factor * gram_margin[offset_lat, offset_lon : offset_lon + tile_count]
            )
            total_pull = (
                total_pull + factor * pull_margin[offset_lat, offset_lon : offset_lon + tile_count]
            )
    system = (members - 1) * jnp.eye(members, dtype=jnp.float32)[None] + total_gram
    frobenius = jnp.sqrt(jnp.sum(system * system, axis=(1, 2)))
    inverse_root = newton_schulz(system / frobenius[:, None, None])
    spread_map = inverse_root * (math.sqrt(members - 1) / jnp.sqrt(frobenius))[:, None, None]
    half_pull = jnp.einsum("tij,tj->ti", inverse_root, total_pull, precision=lax.Precision.HIGHEST)
    shift_weights = (
        jnp.einsum("tij,tj->ti", inverse_root, half_pull, precision=lax.Precision.HIGHEST)
        / frobenius[:, None]
    )
    weights = (spread_map + shift_weights[:, :, None]).astype(jnp.bfloat16)
    state_mean = jnp.sum(tile_block, axis=1, dtype=jnp.float32) / members
    anomaly = (tile_block.astype(jnp.float32) - state_mean[:, None, :]).astype(jnp.bfloat16)
    update = jnp.einsum("tjk,tjc->tkc", weights, anomaly, preferred_element_type=jnp.float32)
    analysed = (state_mean[:, None, :] + update).astype(jnp.bfloat16)
    returned = lax.all_to_all(analysed[None], "mem", split_axis=2, concat_axis=0, tiled=True)
    returned = returned.reshape(strips, tile_count, block_members, 3, tile_columns, strip_rows)
    return jnp.transpose(returned, (2, 3, 1, 4, 0, 5)).reshape(block_members, 3, columns, latitudes)


def solution(mesh):
    in_specs = (
        P("mem", None, "band", None),
        P("band", None),
        P("mem", "band", None),
        P("mem", "band", None),
        P("mem", "band", None),
        P("mem", "band"),
    )
    out_specs = P("mem", None, "band", None)
    return jax.shard_map(
        on_device, mesh=mesh, in_specs=in_specs, out_specs=out_specs, check_vma=False
    )
```

profile of v0, /device:TPU:0, one launch (start us, length us, event | category | flops | bytes accessed | tf_op | source)
XLA Modules:
  0.0 279.9 jit_solution(7164611219929606275)
XLA Ops:
  0.0 2.0 fusion.1
  2.1 5.1 %collective-permute-start = (bf16[32,1,160]{2,0,1:T(8,128)(2,1)S(1)}, bf16[32,1,160]{2,0,1:T(8,128)(2,1)S(1)}, u32[]{:S(2)}, u32[]{:S(2)}) collective-permute-start(bf16[32,1,160]{2,0,1:T(8,128)(2,1)S(1)} %get-tuple-element.15), channel_id=1, source_target_pairs={{1,0},{2,1},{3,2},{0,3},{5,4},{6,5},{7,6},{4,7},{9,8},{10,9},{11,1... | collective-permute-start | bytes 30728 | tf_op jit(solution)/shard_map/ppermute | solution.py:22
  7.2 0.4 pad_convert_fusion
  7.6 1.0 collective-permute-done
  8.6 4.1 %collective-permute-done.1 = bf16[32,1,160]{2,0,1:T(8,128)(2,1)S(1)} collective-permute-done((bf16[32,1,160]{2,0,1:T(8,128)(2,1)S(1)}, bf16[32,1,160]{2,0,1:T(8,128)(2,1)S(1)}, u32[]{:S(2)}, u32[]{:S(2)}) %collective-permute-start.1) | collective-permute-done | bytes 10272 | tf_op jit(solution)/shard_map/ppermute | solution.py:20
  12.7 2.1 fusion.11
  14.9 3.8 %collective-permute-start.3 = (bf16[32,1,160]{2,0,1:T(8,128)(2,1)S(1)}, bf16[32,1,160]{2,0,1:T(8,128)(2,1)S(1)}, u32[]{:S(2)}, u32[]{:S(2)}) collective-permute-start(bf16[32,1,160]{2,0,1:T(8,128)(2,1)S(1)} %get-tuple-element.14), channel_id=1, source_target_pairs={{1,0},{2,1},{3,2},{0,3},{5,4},{6,5},{7,6},{4,7},{9,8},{10,9},{11,1... | collective-permute-start | bytes 30728 | tf_op jit(solution)/shard_map/ppermute | solution.py:22
  18.8 2.1 copy.30
  20.9 4.6 %stack.12 = bf16[32,1,2,30,8,20]{3,2,5,4,0,1:T(2,128)(2,1)S(1)} reshape(bf16[32,60,160]{1,2,0:T(8,128)(2,1)} %copy.30) | data formatting | bytes 1228800 | tf_op jit(solution)/shard_map/stack | solution.py:87
  25.4 1.5 maximum_convert_fusion
  26.9 0.2 slice.164
  27.1 1.6 copy-done.2
  28.7 2.6 fusion.3
  31.4 3.0 %copy.31 = bf16[32,60,160]{1,2,0:T(8,128)(2,1)} copy(bf16[32,60,160]{2,0,1:T(8,128)(2,1)} %get-tuple-element.9) | data formatting | bytes 1228800 | tf_op jit(solution)/shard_map/convert_element_type | solution.py:90
  34.4 5.6 %stack.13 = bf16[32,1,2,30,8,20]{3,2,5,4,0,1:T(2,128)(2,1)} reshape(bf16[32,60,160]{1,2,0:T(8,128)(2,1)} %copy.31) | data formatting | bytes 1228800 | tf_op jit(solution)/shard_map/stack | solution.py:87
  40.0 3.1 %copy.32 = bf16[32,60,160]{1,2,0:T(8,128)(2,1)} copy(bf16[32,60,160]{2,0,1:T(8,128)(2,1)} %get-tuple-element.10) | data formatting | bytes 1228800 | tf_op jit(solution)/shard_map/convert_element_type | solution.py:91
  43.1 5.6 %stack.14 = bf16[32,1,2,30,8,20]{3,2,5,4,0,1:T(2,128)(2,1)} reshape(bf16[32,60,160]{1,2,0:T(8,128)(2,1)} %copy.32) | data formatting | bytes 1228800 | tf_op jit(solution)/shard_map/stack | solution.py:87
  48.7 17.0 %maximum_bitcast_fusion = bf16[8,2,32,3,30,20]{4,1,5,0,2,3:T(2,128)(2,1)} fusion(bf16[32,1,2,30,8,20]{3,2,5,4,0,1:T(2,128)(2,1)} %stack.14, bf16[32,1,2,30,8,20]{3,2,5,4,0,1:T(2,128)(2,1)} %stack.13, bf16[32,1,2,30,8,20]{3,2,5,4,0,1:T(2,128)(2,1)S(1)} %stack.12), kind=kLoop, calls=%fused_computation.1 | loop fusion | flops 1843200 | bytes 3686400 | tf_op jit(solution)/shard_map/transpose | solution.py:98
  65.7 24.9 %copy.33 = bf16[8,2,32,3,30,20]{2,0,5,4,3,1:T(8,128)(2,1)} copy(bf16[8,2,32,3,30,20]{4,1,5,0,2,3:T(2,128)(2,1)} %maximum_bitcast_fusion) | data formatting | bytes 3686400 | tf_op jit(solution)/shard_map/transpose | solution.py:98
  90.6 9.1 %copy.34 = bf16[8,2,32,1800]{3,2,1,0:T(8,128)(2,1)} copy(bf16[8,2,32,1800]{2,0,3,1:T(8,128)(2,1)} %bitcast.114) | data formatting | bytes 3686400 | tf_op jit(solution)/shard_map/reshape | solution.py:98
  99.7 4.0 %all-to-all-start = ((bf16[8,2,32,1800]{3,2,1,0:T(8,128)(2,1)}), bf16[8,2,32,1800]{3,2,1,0:T(8,128)(2,1)S(1)}, u32[]{:S(2)}, u32[]{:S(2)}) async-start(bf16[8,2,32,1800]{3,2,1,0:T(8,128)(2,1)} %copy.34), calls=%async_computation | async-start | bytes 3932160 | tf_op jit(solution)/shard_map/all_to_all | solution.py:101
  103.8 25.0 %all-to-all-done = bf16[8,2,32,1800]{3,2,1,0:T(8,128)(2,1)S(1)} async-done(((bf16[8,2,32,1800]{3,2,1,0:T(8,128)(2,1)}), bf16[8,2,32,1800]{3,2,1,0:T(8,128)(2,1)S(1)}, u32[]{:S(2)}, u32[]{:S(2)}) %all-to-all-start) | async-done | bytes 1843232 | tf_op jit(solution)/shard_map/all_to_all | solution.py:101
  128.8 1.5 copy.35
  130.3 0.5 copy-done
  130.8 2.8 %copy.36 = bf16[2,256,1800]{1,2,0:T(8,128)(2,1)S(1)} copy(bf16[2,256,1800]{2,1,0:T(8,128)(2,1)} %bitcast.118) | data formatting | bytes 3686400 | tf_op jit(solution)/shard_map/squeeze | solution.py:101
  133.6 5.8 %gather_fusion = bf16[1024,256]{1,0:T(8,128)(2,1)S(1)} fusion(bf16[2,256,1800]{1,2,0:T(8,128)(2,1)S(1)} %copy.36, s32[1024]{0:T(1024)S(1)} %bitcast.113), kind=kCustom, calls=%fused_computation | custom fusion | bytes 1056768 | tf_op jit(solution)/shard_map/jit(take_along_axis)/gather | solution.py:103
  139.5 0.2 copy.37
  139.9 0.2 multiply_convert_fusion
  140.1 0.5 collective-permute-start.4
  140.8 2.3 collective-permute-start.9
  143.0 1.9 convert_reduce_fusion
  144.9 7.6 %collective-permute-done.5 = bf16[1,2,256,512]{3,2,1,0:T(8,128)(2,1)S(1)} collective-permute-done((bf16[1,2,256,512]{3,2,1,0:T(8,128)(2,1)S(1)}, bf16[1,2,256,512]{3,2,1,0:T(8,128)(2,1)S(1)}, u32[]{:S(2)}, u32[]{:S(2)}) %collective-permute-start.5) | collective-permute-done | bytes 524320 | tf_op jit(solution)/shard_map/ppermute | solution.py:22
  152.5 1.1 collective-permute-done.4
  153.5 0.2 pad_maximum_fusion.1
  153.7 0.2 fusion.60
  153.9 3.8 %collective-permute-start.7 = (bf16[3,1,256,512]{3,2,1,0:T(8,128)(2,1)S(1)}, bf16[3,1,256,512]{3,2,1,0:T(8,128)(2,1)S(1)}, u32[]{:S(2)}, u32[]{:S(2)}) collective-permute-start(bf16[3,1,256,512]{3,2,1,0:T(8,128)(2,1)S(1)} %get-tuple-element.12), channel_id=1, source_target_pairs={{1,0},{2,1},{3,2},{0,3},{5,4},{6,5},{7,6},{4,7},{9,8},{10,9},{11,1... | collective-permute-start | bytes 2359304 | tf_op jit(solution)/shard_map/ppermute | solution.py:22
  157.9 3.8 %collective-permute-start.11 = (bf16[3,1,512]{2,1,0:T(2,128)(2,1)S(1)}, bf16[3,1,512]{2,1,0:T(2,128)(2,1)S(1)}, u32[]{:S(2)}, u32[]{:S(2)}) collective-permute-start(bf16[3,1,512]{2,1,0:T(2,128)(2,1)S(1)} %get-tuple-element.18), channel_id=1, source_target_pairs={{1,0},{2,1},{3,2},{0,3},{5,4},{6,5},{7,6},{4,7},{9,8},{10,9},{11,1... | collective-permute-start | bytes 9224 | tf_op jit(solution)/shard_map/ppermute | solution.py:22
  161.7 29.6 %collective-permute-done.10 = bf16[3,1,512]{2,1,0:T(2,128)(2,1)S(1)} collective-permute-done((bf16[3,1,512]{2,1,0:T(2,128)(2,1)S(1)}, bf16[3,1,512]{2,1,0:T(2,128)(2,1)S(1)}, u32[]{:S(2)}, u32[]{:S(2)}) %collective-permute-start.10) | collective-permute-done | bytes 3104 | tf_op jit(solution)/shard_map/ppermute | solution.py:20
  191.4 1.3 fusion.58
  192.6 0.5 multiply_reduce_fusion
  193.1 0.7 fusion.17
  193.9 0.7 fusion.35
  194.5 0.6 fusion.29
  195.2 0.7 fusion.16
  195.9 0.7 fusion.65
  196.5 0.7 fusion.64
  197.2 0.7 fusion.15
  197.8 0.7 fusion.67
  198.5 0.7 fusion.66
  199.2 0.7 fusion.14
  199.8 0.7 fusion.68
  200.5 0.7 fusion.69
  201.2 1.3 fusion.36
  202.5 0.7 fusion.13
  203.2 0.7 fusion.70
  203.9 0.5 fusion.56
  204.4 0.6 fusion.54
  205.0 2.2 fusion
  207.2 5.1 %copy.39 = bf16[1,2,256,1800]{3,1,0,2:T(2,128)(2,1)S(1)} copy(bf16[1,2,256,1800]{2,3,1,0:T(8,128)(2,1)} %fusion) | data formatting | bytes 3686400 | tf_op jit(solution)/shard_map/broadcast_in_dim | solution.py:154
  212.3 28.6 %all_to_all.30 = bf16[1,2,256,1800]{3,1,0,2:T(2,128)(2,1)S(1)} all-to-all(bf16[1,2,256,1800]{3,1,0,2:T(2,128)(2,1)S(1)} %copy.39), channel_id=1, replica_groups=mesh['mem'=8,'band'=4] {'mem'}, dimensions={2} | all-to-all | bytes 3686400 | tf_op jit(solution)/shard_map/all_to_all | solution.py:154
  240.9 0.2 copy.40
  241.1 7.6 %copy.41 = bf16[8,1,2,32,1800]{3,0,4,2,1:T(8,128)(2,1)} copy(bf16[8,1,2,32,1800]{4,3,0,2,1:T(8,128)(2,1)S(1)} %bitcast.117) | data formatting | bytes 3686400 | tf_op jit(solution)/shard_map/all_to_all | solution.py:154
  248.6 16.8 %copy.50 = bf16[32,3,2,30,8,20]{5,4,0,3,2,1:T(8,128)(2,1)} copy(bf16[32,3,2,30,8,20]{0,4,5,3,1,2:T(8,128)(2,1)} %bitcast.115) | data formatting | bytes 3686400 | tf_op jit(solution)/shard_map/reshape | solution.py:156
  265.4 14.5 %reshape.287 = bf16[32,3,60,160]{3,0,2,1:T(8,128)(2,1)} reshape(bf16[32,3,2,30,8,20]{5,4,0,3,2,1:T(8,128)(2,1)} %copy.50) | data formatting | bytes 3686400 | tf_op jit(solution)/shard_map/reshape | solution.py:156
  (46 shorter events, 0.9 us)
Async XLA Ops:
  2.1 6.5 %collective-permute-start = (bf16[32,1,160]{2,0,1:T(8,128)(2,1)S(1)}, bf16[32,1,160]{2,0,1:T(8,128)(2,1)S(1)}, u32[]{:S(2)}, u32[]{:S(2)}) collective-permute-start(bf16[32,1,160]{2,0,1:T(8,128)(2,1)S(1)} %get-tuple-element.15), channel_id=1, source_target_pairs={{1,0},{2,1},{3,2},{0,3},{5,4},{6,5},{7,6},{4,7},{9,8},{10,9},{11,1... | collective-permute-start | bytes 30728 | tf_op jit(solution)/shard_map/ppermute | solution.py:22
  7.2 5.5 %collective-permute-start.1 = (bf16[32,1,160]{2,0,1:T(8,128)(2,1)S(1)}, bf16[32,1,160]{2,0,1:T(8,128)(2,1)S(1)}, u32[]{:S(2)}, u32[]{:S(2)}) collective-permute-start(bf16[32,1,160]{2,0,1:T(8,128)(2,1)S(1)} %get-tuple-element.16), channel_id=1, source_target_pairs={{0,1},{1,2},{2,3},{3,0},{4,5},{5,6},{6,7},{7,4},{8,9},{9,10},{10,1... | collective-permute-start | bytes 30728 | tf_op jit(solution)/shard_map/ppermute | solution.py:20
  14.8 4.0 %copy-start.1 = (bf16[32,60,160]{2,0,1:T(8,128)(2,1)}, bf16[32,60,160]{2,0,1:T(8,128)(2,1)S(1)}, u32[]{:S(2)}) copy-start(bf16[32,60,160]{2,0,1:T(8,128)(2,1)S(1)} %fusion.11) | copy-start | bytes 1843204
  14.8 10.6 %collective-permute-start.2 = (bf16[32,1,160]{2,0,1:T(8,128)(2,1)S(1)}, bf16[32,1,160]{2,0,1:T(8,128)(2,1)S(1)}, u32[]{:S(2)}, u32[]{:S(2)}) collective-permute-start(bf16[32,1,160]{2,0,1:T(8,128)(2,1)S(1)} %get-tuple-element.13), channel_id=1, source_target_pairs={{0,1},{1,2},{2,3},{3,0},{4,5},{5,6},{6,7},{7,4},{8,9},{9,10},{10,1... | collective-permute-start | bytes 30728 | tf_op jit(solution)/shard_map/ppermute | solution.py:20
  14.9 10.5 %collective-permute-start.3 = (bf16[32,1,160]{2,0,1:T(8,128)(2,1)S(1)}, bf16[32,1,160]{2,0,1:T(8,128)(2,1)S(1)}, u32[]{:S(2)}, u32[]{:S(2)}) collective-permute-start(bf16[32,1,160]{2,0,1:T(8,128)(2,1)S(1)} %get-tuple-element.14), channel_id=1, source_target_pairs={{1,0},{2,1},{3,2},{0,3},{5,4},{6,5},{7,6},{4,7},{9,8},{10,9},{11,1... | collective-permute-start | bytes 30728 | tf_op jit(solution)/shard_map/ppermute | solution.py:22
  26.9 1.8 copy-start.2
  99.7 4.0 %copy-start.3 = (s32[1,2,512]{2,1,0:T(2,128)S(1)}, s32[1,2,512]{2,1,0:T(2,128)}, u32[]{:S(2)}) copy-start(s32[1,2,512]{2,1,0:T(2,128)} %param.8) | copy-start | bytes 12292
  99.7 29.1 %all-to-all-start = ((bf16[8,2,32,1800]{3,2,1,0:T(8,128)(2,1)}), bf16[8,2,32,1800]{3,2,1,0:T(8,128)(2,1)S(1)}, u32[]{:S(2)}, u32[]{:S(2)}) async-start(bf16[8,2,32,1800]{3,2,1,0:T(8,128)(2,1)} %copy.34), calls=%async_computation | async-start | bytes 3932160 | tf_op jit(solution)/shard_map/all_to_all | solution.py:101
  128.8 2.0 copy-start
  133.6 6.2 %copy-start.4 = (f32[1,2,512]{2,1,0:T(2,128)S(1)}, f32[1,2,512]{2,1,0:T(2,128)}, u32[]{:S(2)}) copy-start(f32[1,2,512]{2,1,0:T(2,128)} %param.10) | copy-start | bytes 12292
  133.6 6.2 %copy-start.6 = (s32[1,2]{1,0:T(1,128)S(1)}, s32[1,2]{1,0:T(1,128)}, u32[]{:S(2)}) copy-start(s32[1,2]{1,0:T(1,128)} %param.11) | copy-start | bytes 28
  139.5 1.2 copy-start.5
  140.1 12.4 %collective-permute-start.5 = (bf16[1,2,256,512]{3,2,1,0:T(8,128)(2,1)S(1)}, bf16[1,2,256,512]{3,2,1,0:T(8,128)(2,1)S(1)}, u32[]{:S(2)}, u32[]{:S(2)}) collective-permute-start(bf16[1,2,256,512]{3,2,1,0:T(8,128)(2,1)S(1)} %multiply_convert_fusion), channel_id=1, source_target_pairs={{4,0},{8,4},{12,8},{16,12},{20,16},{24,20},{28,24},{0,28},{5,1},{9... | collective-permute-start | bytes 1572872 | tf_op jit(solution)/shard_map/ppermute | solution.py:22
  140.1 13.4 %collective-permute-start.4 = (bf16[1,2,256,512]{3,2,1,0:T(8,128)(2,1)S(1)}, bf16[1,2,256,512]{3,2,1,0:T(8,128)(2,1)S(1)}, u32[]{:S(2)}, u32[]{:S(2)}) collective-permute-start(bf16[1,2,256,512]{3,2,1,0:T(8,128)(2,1)S(1)} %multiply_convert_fusion), channel_id=1, source_target_pairs={{0,4},{4,8},{8,12},{12,16},{16,20},{20,24},{24,28},{28,0},{1,5},{5... | collective-permute-start | bytes 1572872 | tf_op jit(solution)/shard_map/ppermute | solution.py:20
  140.8 17.0 %collective-permute-start.9 = (bf16[1,2,512]{2,1,0:T(2,128)(2,1)S(1)}, bf16[1,2,512]{2,1,0:T(2,128)(2,1)S(1)}, u32[]{:S(2)}, u32[]{:S(2)}) collective-permute-start(bf16[1,2,512]{2,1,0:T(2,128)(2,1)S(1)} %fusion.45), channel_id=1, source_target_pairs={{4,0},{8,4},{12,8},{16,12},{20,16},{24,20},{28,24},{0,28},{5,1},{9... | collective-permute-start | bytes 6152 | tf_op jit(solution)/shard_map/ppermute | solution.py:22
  143.0 14.7 %collective-permute-start.8 = (bf16[1,2,512]{2,1,0:T(2,128)(2,1)S(1)}, bf16[1,2,512]{2,1,0:T(2,128)(2,1)S(1)}, u32[]{:S(2)}, u32[]{:S(2)}) collective-permute-start(bf16[1,2,512]{2,1,0:T(2,128)(2,1)S(1)} %fusion.45), channel_id=1, source_target_pairs={{0,4},{4,8},{8,12},{12,16},{16,20},{20,24},{24,28},{28,0},{1,5},{5... | collective-permute-start | bytes 6152 | tf_op jit(solution)/shard_map/ppermute | solution.py:20
  153.9 37.5 %collective-permute-start.6 = (bf16[3,1,256,512]{3,2,1,0:T(8,128)(2,1)S(1)}, bf16[3,1,256,512]{3,2,1,0:T(8,128)(2,1)S(1)}, u32[]{:S(2)}, u32[]{:S(2)}) collective-permute-start(bf16[3,1,256,512]{3,2,1,0:T(8,128)(2,1)S(1)} %get-tuple-element.11), channel_id=1, source_target_pairs={{0,1},{1,2},{2,3},{3,0},{4,5},{5,6},{6,7},{7,4},{8,9},{9,10},{10,1... | collective-permute-start | bytes 2359304 | tf_op jit(solution)/shard_map/ppermute | solution.py:20
  153.9 37.4 %collective-permute-start.7 = (bf16[3,1,256,512]{3,2,1,0:T(8,128)(2,1)S(1)}, bf16[3,1,256,512]{3,2,1,0:T(8,128)(2,1)S(1)}, u32[]{:S(2)}, u32[]{:S(2)}) collective-permute-start(bf16[3,1,256,512]{3,2,1,0:T(8,128)(2,1)S(1)} %get-tuple-element.12), channel_id=1, source_target_pairs={{1,0},{2,1},{3,2},{0,3},{5,4},{6,5},{7,6},{4,7},{9,8},{10,9},{11,1... | collective-permute-start | bytes 2359304 | tf_op jit(solution)/shard_map/ppermute | solution.py:22
  157.8 33.5 %collective-permute-start.10 = (bf16[3,1,512]{2,1,0:T(2,128)(2,1)S(1)}, bf16[3,1,512]{2,1,0:T(2,128)(2,1)S(1)}, u32[]{:S(2)}, u32[]{:S(2)}) collective-permute-start(bf16[3,1,512]{2,1,0:T(2,128)(2,1)S(1)} %get-tuple-element.17), channel_id=1, source_target_pairs={{0,1},{1,2},{2,3},{3,0},{4,5},{5,6},{6,7},{7,4},{8,9},{9,10},{10,1... | collective-permute-start | bytes 9224 | tf_op jit(solution)/shard_map/ppermute | solution.py:20
  157.9 33.4 %collective-permute-start.11 = (bf16[3,1,512]{2,1,0:T(2,128)(2,1)S(1)}, bf16[3,1,512]{2,1,0:T(2,128)(2,1)S(1)}, u32[]{:S(2)}, u32[]{:S(2)}) collective-permute-start(bf16[3,1,512]{2,1,0:T(2,128)(2,1)S(1)} %get-tuple-element.18), channel_id=1, source_target_pairs={{1,0},{2,1},{3,2},{0,3},{5,4},{6,5},{7,6},{4,7},{9,8},{10,9},{11,1... | collective-permute-start | bytes 9224 | tf_op jit(solution)/shard_map/ppermute | solution.py:22
where the time goes:
time: 282 us; the launch traced here: 280 us
  local copies, waits for them, and re-layouts  115 us (41%)
  waiting for transfers between devices  68.4 us (24%)
  other arithmetic  28.9 us (10%)
  blocking collectives  28.6 us (10%)
  starting transfers between devices  23.5 us (8%)
  matrix products  15.1 us (5%)
    ppermute x6, waiting for transfers between devices, padded_2(): lax.ppermute(tail, axis, [(i, (i + 1) % count) for i in range(count)])  34.8 us
    reshape x2, local copies, waits for them, and re-layouts, on_device(): jnp.transpose(returned, (2, 3, 1, 4, 0, 5))  31.3 us
    all_to_all x1, blocking collectives, on_device(): lax.all_to_all(analysed[None], 'mem', split_axis=2, concat_axis=0, tiled=...  28.6 us
    all_to_all x1, waiting for transfers between devices, on_device(): lax.all_to_all(reordered, 'mem', split_axis=0, concat_axis=2, tiled=True)[0]  25 us
    transpose x1, local copies, waits for them, and re-layouts, on_device(): jnp.transpose(reordered, (4, 2, 0, 1, 3, 5))  24.9 us
    ppermute x6, starting transfers between devices, padded_2(): lax.ppermute(head, axis, [((i + 1) % count, i) for i in range(count)])  18.8 us
    transpose x1, other arithmetic, on_device(): jnp.transpose(reordered, (4, 2, 0, 1, 3, 5))  17 us
    another operation x3, local copies, waits for them, and re-layouts, on_device(): jnp.stack([surface_elevation_cast, revised_zonal_velocity.astype(jnp.bflo...  15.8 us
  transfers between devices with their start and end apart: 13, of which 6 were waited for; matrix products, arithmetic and copies ran while one was open for 3% of the time, Pallas kernels for 0%

commit v1 on v0

--- a/solution.py
+++ b/solution.py
@@ -8,6 +8,13 @@
 half_step = 0.1
 coriolis_scale = 0.3
 neighbour_weight = 0.75
+
+
+def stacked_exchange(value, mesh_axis, split, join):
+    size = lax.axis_size(mesh_axis)
+    blocks = jnp.stack(jnp.split(value, size, axis=split), axis=0)
+    blocks = lax.all_to_all(blocks, mesh_axis, split_axis=0, concat_axis=0)
+    return jnp.concatenate(blocks, axis=join)
 
 
 def padded_2(cells, sides, width):
@@ -98,7 +105,7 @@
     reordered = jnp.transpose(reordered, (4, 2, 0, 1, 3, 5)).reshape(
         strips, tile_count, block_members, tile_cells
     )
-    tile_block = lax.all_to_all(reordered, "mem", split_axis=0, concat_axis=2, tiled=True)[0]
+    tile_block = stacked_exchange(reordered, "mem", 0, 2)[0]
     cells_here = observed_cell[0]
     values = jnp.take_along_axis(tile_block, cells_here[:, None, :], axis=2)
     observed_mean = jnp.sum(values, axis=1, dtype=jnp.float32) / members

time: 282 us -> 308 us (1.092)
  local copies, waits for them, and re-layouts: 115 us -> 137 us
    split x0 -> x9, local copies, waits for them, and re-layouts: none -> 32.7 us  [stacked_exchange(): blocks = jnp.stack(jnp.split(value, size, axis=split), axis=0)]
    transpose x1 -> x0, local copies, waits for them, and re-layouts: 24.9 us -> none  [on_device(): jnp.transpose(reordered, (4, 2, 0, 1, 3, 5))]
    another operation x0 -> x10, local copies, waits for them, and re-layouts: none -> 20.7 us  [the longest x9 17.8 us: stacked_exchange(): blocks = jnp.stack(jnp.split(value, size, axis=split), axis=0)]
    reshape x1, local copies, waits for them, and re-layouts: 9.05 us -> 2.97 us  [stacked_exchange(): return jnp.concatenate(blocks, axis=join)]
    unnamed x15 -> x32, local copies, waits for them, and re-layouts: 2.09 us -> 6.64 us
where the time goes in v1:
time: 308 us; the launch traced here: 303 us
  local copies, waits for them, and re-layouts  137 us (44%)
  waiting for transfers between devices  68.3 us (22%)
  blocking collectives  28.6 us (9%)
  other arithmetic  28.2 us (9%)
  starting transfers between devices  24.7 us (8%)
  matrix products  15.2 us (5%)
    ppermute x6, waiting for transfers between devices, padded_2(): lax.ppermute(tail, axis, [(i, (i + 1) % count) for i in range(count)])  34.6 us
    split x9, local copies, waits for them, and re-layouts, stacked_exchange(): blocks = jnp.stack(jnp.split(value, size, axis=split), axis=0)  32.7 us
    reshape x2, local copies, waits for them, and re-layouts, on_device(): jnp.transpose(returned, (2, 3, 1, 4, 0, 5))  31.3 us
    all_to_all x1, blocking collectives, on_device(): lax.all_to_all(analysed[None], 'mem', split_axis=2, concat_axis=0, tiled=...  28.6 us
    all_to_all x1, waiting for transfers between devices, stacked_exchange(): blocks = lax.all_to_all(blocks, mesh_axis, split_axis=0, concat_axis=0)  25.1 us
    ppermute x6, starting transfers between devices, padded_2(): lax.ppermute(head, axis, [((i + 1) % count, i) for i in range(count)])  19.6 us
    another operation x9, local copies, waits for them, and re-layouts, stacked_exchange(): blocks = jnp.stack(jnp.split(value, size, axis=split), axis=0)  17.8 us
    transpose x1, other arithmetic, on_device(): jnp.transpose(reordered, (4, 2, 0, 1, 3, 5))  16.2 us
  transfers between devices with their start and end apart: 13, of which 6 were waited for; matrix products, arithmetic and copies ran while one was open for 3% of the time, Pallas kernels for 0%

profile of v1, /device:TPU:0, one launch (start us, length us, event | category | flops | bytes accessed | tf_op | source)
XLA Modules:
  0.0 303.4 jit_solution(4088305750039314317)
XLA Ops:
  0.0 2.0 fusion.1
  2.1 5.1 %collective-permute-start = (bf16[32,1,160]{2,0,1:T(8,128)(2,1)S(1)}, bf16[32,1,160]{2,0,1:T(8,128)(2,1)S(1)}, u32[]{:S(2)}, u32[]{:S(2)}) collective-permute-start(bf16[32,1,160]{2,0,1:T(8,128)(2,1)S(1)} %get-tuple-element.23), channel_id=1, source_target_pairs={{1,0},{2,1},{3,2},{0,3},{5,4},{6,5},{7,6},{4,7},{9,8},{10,9},{11,1... | collective-permute-start | bytes 30728 | tf_op jit(solution)/shard_map/ppermute | solution.py:29
  7.6 1.0 collective-permute-done
  8.6 4.1 %collective-permute-done.1 = bf16[32,1,160]{2,0,1:T(8,128)(2,1)S(1)} collective-permute-done((bf16[32,1,160]{2,0,1:T(8,128)(2,1)S(1)}, bf16[32,1,160]{2,0,1:T(8,128)(2,1)S(1)}, u32[]{:S(2)}, u32[]{:S(2)}) %collective-permute-start.1) | collective-permute-done | bytes 10272 | tf_op jit(solution)/shard_map/ppermute | solution.py:27
  12.7 2.1 fusion.11
  14.9 4.3 %collective-permute-start.3 = (bf16[32,1,160]{2,0,1:T(8,128)(2,1)S(1)}, bf16[32,1,160]{2,0,1:T(8,128)(2,1)S(1)}, u32[]{:S(2)}, u32[]{:S(2)}) collective-permute-start(bf16[32,1,160]{2,0,1:T(8,128)(2,1)S(1)} %get-tuple-element.22), channel_id=1, source_target_pairs={{1,0},{2,1},{3,2},{0,3},{5,4},{6,5},{7,6},{4,7},{9,8},{10,9},{11,1... | collective-permute-start | bytes 30728 | tf_op jit(solution)/shard_map/ppermute | solution.py:29
  19.3 2.1 copy.53
  21.4 4.6 %stack.39 = bf16[32,1,2,30,8,20]{3,2,5,4,0,1:T(2,128)(2,1)S(1)} reshape(bf16[32,60,160]{1,2,0:T(8,128)(2,1)} %copy.53) | data formatting | bytes 1228800 | tf_op jit(solution)/shard_map/stack | solution.py:94
  25.9 1.5 maximum_convert_fusion
  27.6 1.6 copy-done.1
  29.2 2.6 fusion.3
  31.9 3.0 %copy.54 = bf16[32,60,160]{1,2,0:T(8,128)(2,1)} copy(bf16[32,60,160]{2,0,1:T(8,128)(2,1)} %get-tuple-element.17) | data formatting | bytes 1228800 | tf_op jit(solution)/shard_map/convert_element_type | solution.py:97
  34.9 5.6 %stack.40 = bf16[32,1,2,30,8,20]{3,2,5,4,0,1:T(2,128)(2,1)} reshape(bf16[32,60,160]{1,2,0:T(8,128)(2,1)} %copy.54) | data formatting | bytes 1228800 | tf_op jit(solution)/shard_map/stack | solution.py:94
  40.5 3.0 %copy.55 = bf16[32,60,160]{1,2,0:T(8,128)(2,1)} copy(bf16[32,60,160]{2,0,1:T(8,128)(2,1)} %get-tuple-element.18) | data formatting | bytes 1228800 | tf_op jit(solution)/shard_map/convert_element_type | solution.py:98
  43.6 5.6 %stack.41 = bf16[32,1,2,30,8,20]{3,2,5,4,0,1:T(2,128)(2,1)} reshape(bf16[32,60,160]{1,2,0:T(8,128)(2,1)} %copy.55) | data formatting | bytes 1228800 | tf_op jit(solution)/shard_map/stack | solution.py:94
  49.2 16.2 %maximum_bitcast_fusion = bf16[8,2,32,3,30,20]{4,1,5,0,2,3:T(2,128)(2,1)S(1)} fusion(bf16[32,1,2,30,8,20]{3,2,5,4,0,1:T(2,128)(2,1)} %stack.41, bf16[32,1,2,30,8,20]{3,2,5,4,0,1:T(2,128)(2,1)} %stack.40, bf16[32,1,2,30,8,20]{3,2,5,4,0,1:T(2,128)(2,1)S(1)} %stack.39), kind=kLoop, calls=%fused_computation.1 | loop fusion | flops 1843200 | bytes 3686400 | tf_op jit(solution)/shard_map/transpose | solution.py:105
  65.4 9.2 %fusion.60 = (bf16[1,2,32,3,30,20]{4,1,5,0,2,3:T(2,128)(2,1)}, bf16[1,2,32,3,30,20]{4,1,5,0,2,3:T(2,128)(2,1)}, bf16[1,2,32,3,30,20]{4,1,5,0,2,3:T(2,128)(2,1)},...) fusion(bf16[8,2,32,3,30,20]{4,1,5,0,2,3:T(2,128)(2,1)S(1)} %max, ...), kind=kLoop, calls=%fused_computation.133 | loop fusion | bytes 3686400 | tf_op jit(solution)/shard_map/split | solution.py:15
  74.6 3.4 %copy.63 = bf16[1,2,32,3,30,20]{5,4,3,2,1,0:T(8,128)(2,1)S(1)} copy(bf16[1,2,32,3,30,20]{4,1,5,0,2,3:T(2,128)(2,1)} %get-tuple-element.7) | data formatting | bytes 460800 | tf_op jit(solution)/shard_map/split | solution.py:15
  78.0 2.3 stack.50
  80.3 3.2 %copy.62 = bf16[1,2,32,3,30,20]{5,4,3,2,1,0:T(8,128)(2,1)S(1)} copy(bf16[1,2,32,3,30,20]{4,1,5,0,2,3:T(2,128)(2,1)} %get-tuple-element.8) | data formatting | bytes 460800 | tf_op jit(solution)/shard_map/split | solution.py:15
  83.6 2.3 stack.49
  85.9 3.2 %copy.61 = bf16[1,2,32,3,30,20]{5,4,3,2,1,0:T(8,128)(2,1)S(1)} copy(bf16[1,2,32,3,30,20]{4,1,5,0,2,3:T(2,128)(2,1)} %get-tuple-element.9) | data formatting | bytes 460800 | tf_op jit(solution)/shard_map/split | solution.py:15
  89.1 2.3 stack.48
  91.5 3.2 %copy.60 = bf16[1,2,32,3,30,20]{5,4,3,2,1,0:T(8,128)(2,1)S(1)} copy(bf16[1,2,32,3,30,20]{4,1,5,0,2,3:T(2,128)(2,1)} %get-tuple-element.10) | data formatting | bytes 460800 | tf_op jit(solution)/shard_map/split | solution.py:15
  94.7 2.3 stack.47
  97.0 3.2 %copy.59 = bf16[1,2,32,3,30,20]{5,4,3,2,1,0:T(8,128)(2,1)S(1)} copy(bf16[1,2,32,3,30,20]{4,1,5,0,2,3:T(2,128)(2,1)} %get-tuple-element.11) | data formatting | bytes 460800 | tf_op jit(solution)/shard_map/split | solution.py:15
  100.3 2.3 stack.46
  102.6 3.2 %copy.58 = bf16[1,2,32,3,30,20]{5,4,3,2,1,0:T(8,128)(2,1)S(1)} copy(bf16[1,2,32,3,30,20]{4,1,5,0,2,3:T(2,128)(2,1)} %get-tuple-element.12) | data formatting | bytes 460800 | tf_op jit(solution)/shard_map/split | solution.py:15
  105.8 2.3 stack.45
  108.2 2.1 copy.57
  110.2 1.6 stack.44
  111.8 1.8 copy.56
  113.7 1.6 stack.43
  115.3 0.7 constant_dynamic-update-slice_fusion.7
  116.1 0.7 constant_dynamic-update-slice_fusion.6
  116.8 0.7 constant_dynamic-update-slice_fusion.5
  117.5 0.7 constant_dynamic-update-slice_fusion.4
  118.2 0.7 constant_dynamic-update-slice_fusion.3
  118.9 0.7 constant_dynamic-update-slice_fusion.2
  119.6 0.7 constant_dynamic-update-slice_fusion.1
  120.3 0.7 constant_dynamic-update-slice_fusion
  121.0 4.5 %all-to-all-start = ((bf16[8,1,2,32,1800]{4,3,2,1,0:T(8,128)(2,1)}), bf16[8,1,2,32,1800]{4,3,2,1,0:T(8,128)(2,1)}, u32[]{:S(2)}, u32[]{:S(2)}) async-start(bf16[8,1,2,32,1800]{4,3,2,1,0:T(8,128)(2,1)} %constant_dynamic-update-slice_fusion), calls=%async_computation | async-start | bytes 3932160 | tf_op jit(solution)/shard_map/all_to_all | solution.py:16
  125.7 25.1 %all-to-all-done = bf16[8,1,2,32,1800]{4,3,2,1,0:T(8,128)(2,1)} async-done(((bf16[8,1,2,32,1800]{4,3,2,1,0:T(8,128)(2,1)}), bf16[8,1,2,32,1800]{4,3,2,1,0:T(8,128)(2,1)}, u32[]{:S(2)}, u32[]{:S(2)}) %all-to-all-start) | async-done | bytes 1843232 | tf_op jit(solution)/shard_map/all_to_all | solution.py:16
  150.8 3.0 copy.64
  153.7 2.8 copy.65
  156.6 5.8 %gather_fusion = bf16[1024,256]{1,0:T(8,128)(2,1)S(1)} fusion(bf16[2,256,1800]{1,2,0:T(8,128)(2,1)S(1)} %copy.65, s32[1024]{0:T(1024)S(1)} %bitcast.110), kind=kCustom, calls=%fused_computation | custom fusion | bytes 1056768 | tf_op jit(solution)/shard_map/jit(take_along_axis)/gather | solution.py:110
  163.7 2.3 collective-permute-start.9
  166.0 1.9 convert_reduce_fusion
  167.9 7.6 %collective-permute-done.5 = bf16[1,2,256,512]{3,2,1,0:T(8,128)(2,1)S(1)} collective-permute-done((bf16[1,2,256,512]{3,2,1,0:T(8,128)(2,1)S(1)}, bf16[1,2,256,512]{3,2,1,0:T(8,128)(2,1)S(1)}, u32[]{:S(2)}, u32[]{:S(2)}) %collective-permute-start.5) | collective-permute-done | bytes 524320 | tf_op jit(solution)/shard_map/ppermute | solution.py:29
  175.4 1.1 collective-permute-done.4
  176.9 3.8 %collective-permute-start.7 = (bf16[3,1,256,512]{3,2,1,0:T(8,128)(2,1)S(1)}, bf16[3,1,256,512]{3,2,1,0:T(8,128)(2,1)S(1)}, u32[]{:S(2)}, u32[]{:S(2)}) collective-permute-start(bf16[3,1,256,512]{3,2,1,0:T(8,128)(2,1)S(1)} %get-tuple-element.20), channel_id=1, source_target_pairs={{1,0},{2,1},{3,2},{0,3},{5,4},{6,5},{7,6},{4,7},{9,8},{10,9},{11,1... | collective-permute-start | bytes 2359304 | tf_op jit(solution)/shard_map/ppermute | solution.py:29
  180.8 4.0 %collective-permute-start.11 = (bf16[3,1,512]{2,1,0:T(2,128)(2,1)S(1)}, bf16[3,1,512]{2,1,0:T(2,128)(2,1)S(1)}, u32[]{:S(2)}, u32[]{:S(2)}) collective-permute-start(bf16[3,1,512]{2,1,0:T(2,128)(2,1)S(1)} %get-tuple-element.26), channel_id=1, source_target_pairs={{1,0},{2,1},{3,2},{0,3},{5,4},{6,5},{7,6},{4,7},{9,8},{10,9},{11,1... | collective-permute-start | bytes 9224 | tf_op jit(solution)/shard_map/ppermute | solution.py:29
  184.8 29.4 %collective-permute-done.10 = bf16[3,1,512]{2,1,0:T(2,128)(2,1)S(1)} collective-permute-done((bf16[3,1,512]{2,1,0:T(2,128)(2,1)S(1)}, bf16[3,1,512]{2,1,0:T(2,128)(2,1)S(1)}, u32[]{:S(2)}, u32[]{:S(2)}) %collective-permute-start.10) | collective-permute-done | bytes 3104 | tf_op jit(solution)/shard_map/ppermute | solution.py:27
  214.3 1.3 fusion.58
  216.1 0.7 fusion.17
  216.8 0.7 fusion.35
  224.1 1.4 fusion.36
  225.5 0.7 fusion.13
  228.1 2.2 fusion
  230.2 5.1 %copy.68 = bf16[1,2,256,1800]{3,1,0,2:T(2,128)(2,1)S(1)} copy(bf16[1,2,256,1800]{2,3,1,0:T(8,128)(2,1)} %fusion) | data formatting | bytes 3686400 | tf_op jit(solution)/shard_map/broadcast_in_dim | solution.py:161
  235.3 28.6 %all_to_all.20 = bf16[1,2,256,1800]{3,1,0,2:T(2,128)(2,1)S(1)} all-to-all(bf16[1,2,256,1800]{3,1,0,2:T(2,128)(2,1)S(1)} %copy.68), channel_id=1, replica_groups=mesh['mem'=8,'band'=4] {'mem'}, dimensions={2} | all-to-all | bytes 3686400 | tf_op jit(solution)/shard_map/all_to_all | solution.py:161
  264.1 7.5 %copy.70 = bf16[8,1,2,32,1800]{3,0,4,2,1:T(8,128)(2,1)} copy(bf16[8,1,2,32,1800]{4,3,0,2,1:T(8,128)(2,1)S(1)} %bitcast.112) | data formatting | bytes 3686400 | tf_op jit(solution)/shard_map/all_to_all | solution.py:161
  271.6 16.8 %copy.79 = bf16[32,3,2,30,8,20]{5,4,0,3,2,1:T(8,128)(2,1)} copy(bf16[32,3,2,30,8,20]{0,4,5,3,1,2:T(8,128)(2,1)} %bitcast.111) | data formatting | bytes 3686400 | tf_op jit(solution)/shard_map/reshape | solution.py:163
  288.4 14.5 %reshape.303 = bf16[32,3,60,160]{3,0,2,1:T(8,128)(2,1)} reshape(bf16[32,3,2,30,8,20]{5,4,0,3,2,1:T(8,128)(2,1)} %copy.79) | data formatting | bytes 3686400 | tf_op jit(solution)/shard_map/reshape | solution.py:163
  (79 shorter events, 11.7 us)
Async XLA Ops:
  2.1 6.5 %collective-permute-start = (bf16[32,1,160]{2,0,1:T(8,128)(2,1)S(1)}, bf16[32,1,160]{2,0,1:T(8,128)(2,1)S(1)}, u32[]{:S(2)}, u32[]{:S(2)}) collective-permute-start(bf16[32,1,160]{2,0,1:T(8,128)(2,1)S(1)} %get-tuple-element.23), channel_id=1, source_target_pairs={{1,0},{2,1},{3,2},{0,3},{5,4},{6,5},{7,6},{4,7},{9,8},{10,9},{11,1... | collective-permute-start | bytes 30728 | tf_op jit(solution)/shard_map/ppermute | solution.py:29
  7.2 5.5 %collective-permute-start.1 = (bf16[32,1,160]{2,0,1:T(8,128)(2,1)S(1)}, bf16[32,1,160]{2,0,1:T(8,128)(2,1)S(1)}, u32[]{:S(2)}, u32[]{:S(2)}) collective-permute-start(bf16[32,1,160]{2,0,1:T(8,128)(2,1)S(1)} %get-tuple-element.24), channel_id=1, source_target_pairs={{0,1},{1,2},{2,3},{3,0},{4,5},{5,6},{6,7},{7,4},{8,9},{9,10},{10,1... | collective-permute-start | bytes 30728 | tf_op jit(solution)/shard_map/ppermute | solution.py:27
  14.8 4.5 %copy-start = (bf16[32,60,160]{2,0,1:T(8,128)(2,1)}, bf16[32,60,160]{2,0,1:T(8,128)(2,1)S(1)}, u32[]{:S(2)}) copy-start(bf16[32,60,160]{2,0,1:T(8,128)(2,1)S(1)} %fusion.11) | copy-start | bytes 1843204
  14.8 11.1 %collective-permute-start.2 = (bf16[32,1,160]{2,0,1:T(8,128)(2,1)S(1)}, bf16[32,1,160]{2,0,1:T(8,128)(2,1)S(1)}, u32[]{:S(2)}, u32[]{:S(2)}) collective-permute-start(bf16[32,1,160]{2,0,1:T(8,128)(2,1)S(1)} %get-tuple-element.21), channel_id=1, source_target_pairs={{0,1},{1,2},{2,3},{3,0},{4,5},{5,6},{6,7},{7,4},{8,9},{9,10},{10,1... | collective-permute-start | bytes 30728 | tf_op jit(solution)/shard_map/ppermute | solution.py:27
  14.9 11.0 %collective-permute-start.3 = (bf16[32,1,160]{2,0,1:T(8,128)(2,1)S(1)}, bf16[32,1,160]{2,0,1:T(8,128)(2,1)S(1)}, u32[]{:S(2)}, u32[]{:S(2)}) collective-permute-start(bf16[32,1,160]{2,0,1:T(8,128)(2,1)S(1)} %get-tuple-element.22), channel_id=1, source_target_pairs={{1,0},{2,1},{3,2},{0,3},{5,4},{6,5},{7,6},{4,7},{9,8},{10,9},{11,1... | collective-permute-start | bytes 30728 | tf_op jit(solution)/shard_map/ppermute | solution.py:29
  27.4 1.8 copy-start.1
  113.7 3.1 %copy-start.7 = (bf16[1,1,2,32,1800]{4,3,2,1,0:T(8,128)(2,1)S(1)}, bf16[1,1,2,32,1800]{4,3,2,1,0:T(8,128)(2,1)}, u32[]{:S(2)}) copy-start(bf16[1,1,2,32,1800]{4,3,2,1,0:T(8,128)(2,1)} %stack.45) | copy-start | bytes 691204
  113.7 3.8 %copy-start.6 = (bf16[1,1,2,32,1800]{4,3,2,1,0:T(8,128)(2,1)S(1)}, bf16[1,1,2,32,1800]{4,3,2,1,0:T(8,128)(2,1)}, u32[]{:S(2)}) copy-start(bf16[1,1,2,32,1800]{4,3,2,1,0:T(8,128)(2,1)} %stack.46) | copy-start | bytes 691204
  113.7 4.5 %copy-start.5 = (bf16[1,1,2,32,1800]{4,3,2,1,0:T(8,128)(2,1)S(1)}, bf16[1,1,2,32,1800]{4,3,2,1,0:T(8,128)(2,1)}, u32[]{:S(2)}) copy-start(bf16[1,1,2,32,1800]{4,3,2,1,0:T(8,128)(2,1)} %stack.47) | copy-start | bytes 691204
  113.7 5.2 %copy-start.4 = (bf16[1,1,2,32,1800]{4,3,2,1,0:T(8,128)(2,1)S(1)}, bf16[1,1,2,32,1800]{4,3,2,1,0:T(8,128)(2,1)}, u32[]{:S(2)}) copy-start(bf16[1,1,2,32,1800]{4,3,2,1,0:T(8,128)(2,1)} %stack.48) | copy-start | bytes 691204
  113.7 5.9 %copy-start.3 = (bf16[1,1,2,32,1800]{4,3,2,1,0:T(8,128)(2,1)S(1)}, bf16[1,1,2,32,1800]{4,3,2,1,0:T(8,128)(2,1)}, u32[]{:S(2)}) copy-start(bf16[1,1,2,32,1800]{4,3,2,1,0:T(8,128)(2,1)} %stack.49) | copy-start | bytes 691204
  115.3 5.0 %copy-start.2 = (bf16[1,1,2,32,1800]{4,3,2,1,0:T(8,128)(2,1)S(1)}, bf16[1,1,2,32,1800]{4,3,2,1,0:T(8,128)(2,1)}, u32[]{:S(2)}) copy-start(bf16[1,1,2,32,1800]{4,3,2,1,0:T(8,128)(2,1)} %stack.50) | copy-start | bytes 691204
  121.0 4.5 %copy-start.8 = (s32[1,2,512]{2,1,0:T(2,128)S(1)}, s32[1,2,512]{2,1,0:T(2,128)}, u32[]{:S(2)}) copy-start(s32[1,2,512]{2,1,0:T(2,128)} %param.8) | copy-start | bytes 12292
  121.0 29.7 %all-to-all-start = ((bf16[8,1,2,32,1800]{4,3,2,1,0:T(8,128)(2,1)}), bf16[8,1,2,32,1800]{4,3,2,1,0:T(8,128)(2,1)}, u32[]{:S(2)}, u32[]{:S(2)}) async-start(bf16[8,1,2,32,1800]{4,3,2,1,0:T(8,128)(2,1)} %constant_dynamic-update-slice_fusion), calls=%async_computation | async-start | bytes 3932160 | tf_op jit(solution)/shard_map/all_to_all | solution.py:16
  156.6 6.2 %copy-start.9 = (f32[1,2,512]{2,1,0:T(2,128)S(1)}, f32[1,2,512]{2,1,0:T(2,128)}, u32[]{:S(2)}) copy-start(f32[1,2,512]{2,1,0:T(2,128)} %param.10) | copy-start | bytes 12292
  156.6 6.2 %copy-start.11 = (s32[1,2]{1,0:T(1,128)S(1)}, s32[1,2]{1,0:T(1,128)}, u32[]{:S(2)}) copy-start(s32[1,2]{1,0:T(1,128)} %param.11) | copy-start | bytes 28
  162.4 1.2 copy-start.10
  163.1 12.4 %collective-permute-start.5 = (bf16[1,2,256,512]{3,2,1,0:T(8,128)(2,1)S(1)}, bf16[1,2,256,512]{3,2,1,0:T(8,128)(2,1)S(1)}, u32[]{:S(2)}, u32[]{:S(2)}) collective-permute-start(bf16[1,2,256,512]{3,2,1,0:T(8,128)(2,1)S(1)} %multiply_convert_fusion), channel_id=1, source_target_pairs={{4,0},{8,4},{12,8},{16,12},{20,16},{24,20},{28,24},{0,28},{5,1},{9... | collective-permute-start | bytes 1572872 | tf_op jit(solution)/shard_map/ppermute | solution.py:29
  163.1 13.4 %collective-permute-start.4 = (bf16[1,2,256,512]{3,2,1,0:T(8,128)(2,1)S(1)}, bf16[1,2,256,512]{3,2,1,0:T(8,128)(2,1)S(1)}, u32[]{:S(2)}, u32[]{:S(2)}) collective-permute-start(bf16[1,2,256,512]{3,2,1,0:T(8,128)(2,1)S(1)} %multiply_convert_fusion), channel_id=1, source_target_pairs={{0,4},{4,8},{8,12},{12,16},{16,20},{20,24},{24,28},{28,0},{1,5},{5... | collective-permute-start | bytes 1572872 | tf_op jit(solution)/shard_map/ppermute | solution.py:27
  163.7 16.9 %collective-permute-start.9 = (bf16[1,2,512]{2,1,0:T(2,128)(2,1)S(1)}, bf16[1,2,512]{2,1,0:T(2,128)(2,1)S(1)}, u32[]{:S(2)}, u32[]{:S(2)}) collective-permute-start(bf16[1,2,512]{2,1,0:T(2,128)(2,1)S(1)} %fusion.45), channel_id=1, source_target_pairs={{4,0},{8,4},{12,8},{16,12},{20,16},{24,20},{28,24},{0,28},{5,1},{9... | collective-permute-start | bytes 6152 | tf_op jit(solution)/shard_map/ppermute | solution.py:29
  166.0 14.7 %collective-permute-start.8 = (bf16[1,2,512]{2,1,0:T(2,128)(2,1)S(1)}, bf16[1,2,512]{2,1,0:T(2,128)(2,1)S(1)}, u32[]{:S(2)}, u32[]{:S(2)}) collective-permute-start(bf16[1,2,512]{2,1,0:T(2,128)(2,1)S(1)} %fusion.45), channel_id=1, source_target_pairs={{0,4},{4,8},{8,12},{12,16},{16,20},{20,24},{24,28},{28,0},{1,5},{5... | collective-permute-start | bytes 6152 | tf_op jit(solution)/shard_map/ppermute | solution.py:27
  176.8 37.5 %collective-permute-start.6 = (bf16[3,1,256,512]{3,2,1,0:T(8,128)(2,1)S(1)}, bf16[3,1,256,512]{3,2,1,0:T(8,128)(2,1)S(1)}, u32[]{:S(2)}, u32[]{:S(2)}) collective-permute-start(bf16[3,1,256,512]{3,2,1,0:T(8,128)(2,1)S(1)} %get-tuple-element.19), channel_id=1, source_target_pairs={{0,1},{1,2},{2,3},{3,0},{4,5},{5,6},{6,7},{7,4},{8,9},{9,10},{10,1... | collective-permute-start | bytes 2359304 | tf_op jit(solution)/shard_map/ppermute | solution.py:27
  176.9 37.4 %collective-permute-start.7 = (bf16[3,1,256,512]{3,2,1,0:T(8,128)(2,1)S(1)}, bf16[3,1,256,512]{3,2,1,0:T(8,128)(2,1)S(1)}, u32[]{:S(2)}, u32[]{:S(2)}) collective-permute-start(bf16[3,1,256,512]{3,2,1,0:T(8,128)(2,1)S(1)} %get-tuple-element.20), channel_id=1, source_target_pairs={{1,0},{2,1},{3,2},{0,3},{5,4},{6,5},{7,6},{4,7},{9,8},{10,9},{11,1... | collective-permute-start | bytes 2359304 | tf_op jit(solution)/shard_map/ppermute | solution.py:29
  180.7 33.5 %collective-permute-start.10 = (bf16[3,1,512]{2,1,0:T(2,128)(2,1)S(1)}, bf16[3,1,512]{2,1,0:T(2,128)(2,1)S(1)}, u32[]{:S(2)}, u32[]{:S(2)}) collective-permute-start(bf16[3,1,512]{2,1,0:T(2,128)(2,1)S(1)} %get-tuple-element.25), channel_id=1, source_target_pairs={{0,1},{1,2},{2,3},{3,0},{4,5},{5,6},{6,7},{7,4},{8,9},{9,10},{10,1... | collective-permute-start | bytes 9224 | tf_op jit(solution)/shard_map/ppermute | solution.py:27
  180.8 33.4 %collective-permute-start.11 = (bf16[3,1,512]{2,1,0:T(2,128)(2,1)S(1)}, bf16[3,1,512]{2,1,0:T(2,128)(2,1)S(1)}, u32[]{:S(2)}, u32[]{:S(2)}) collective-permute-start(bf16[3,1,512]{2,1,0:T(2,128)(2,1)S(1)} %get-tuple-element.26), channel_id=1, source_target_pairs={{1,0},{2,1},{3,2},{0,3},{5,4},{6,5},{7,6},{4,7},{9,8},{10,9},{11,1... | collective-permute-start | bytes 9224 | tf_op jit(solution)/shard_map/ppermute | solution.py:29
